TPU v7x, 256 devices: a whole 4x4x8 slice. The times are simulated.
256 devices in a mesh: ctx: 16 (over y, x), grp: 16 (over z, core).
Axes of the slice: x: 4, y: 4, z: 8, core: 2. Of those that a mesh axis runs over, the one named last changes fastest.
Arguments:
- q_in: bfloat16 [2048, 8192], P('ctx', 'grp'), may hold values from -170 to 170
- k_in: bfloat16 [2048, 8192], P('ctx', 'grp'), may hold values from -6 to 6
- v_in: bfloat16 [2048, 8192], P('ctx', 'grp'), may hold values from -6 to 6
- fir: float32 [3, 3, 8192], P(None, None, 'grp'), may hold values from -3 to 3
- skip: float32 [8192], P('grp'), may hold values from 0.2 to 1
- taps: bfloat16 [64, 2048], P('grp'), may hold values from -0.25 to 0.25
- segments: int32 [2048], P('ctx'), may hold values from 0 to 1, never falling along the last dimension, each value on 1 to 1920 neighbouring positions
- gain: float32 [8192], P('grp'), may hold values from 0.1 to 1.9
Outputs:
- mixed: bfloat16 [2048, 8192], P('ctx', 'grp')
All inputs are finite; a program needn't handle non-finite values.
Results may differ from a plain program's by a relative error of at most 0.0085.
Values may be sent and summed in bfloat16 or wider, within the bound.
No kernel may reach another device: no remote copies, remote signals or barrier semaphores. Data moves between devices by JAX's collectives and lax.ppermute only.
A program may use at most 64 MiB of HBM per device.

v0:
```python
import jax
import jax.numpy as jnp
from jax import lax
from jax.sharding import PartitionSpec as P

D = 8192
GW = 128


def shifted(value, axis, by):
    peers = lax.axis_size(axis)
    pairs = [(i, i + by) for i in range(peers) if 0 <= i + by < peers]
    return lax.ppermute(value, axis, pairs)


def band_rect(padded_taps, pad_left, lag_base, rows, cols):
    length = rows + cols - 1
    window = lax.dynamic_slice_in_dim(padded_taps, lag_base - cols + 1 + pad_left, length, 0)
    flipped = jnp.concatenate([window[::-1], jnp.zeros((1,), padded_taps.dtype)])
    tiled = jnp.tile(flipped, rows)[: rows * length].reshape(rows, length)
    return tiled[:, rows - 1 :]


def token_conv(product_kv, taps, all_segs, segments):
    rows_dev, width = product_kv.shape
    groups_local = width // GW
    total_rows = all_segs.shape[0]
    my_start = lax.axis_index("ctx") * rows_dev
    margin = jnp.zeros((total_rows,), taps.dtype)
    padded_taps = [jnp.concatenate([margin, taps[group], margin]) for group in range(groups_local)]
    empty = jnp.zeros((rows_dev, width), jnp.float32)
    piece = lax.all_gather(product_kv, "ctx", axis=0, tiled=True)
    count = piece.shape[0]
    needed = (jnp.int32(0) <= my_start + rows_dev - 1) & (all_segs[-1] >= segments[0])
    allowed = segments[:, None] == all_segs[None, :]

    def work(total):
        parts_out = []
        for group in range(groups_local):
            matrix = band_rect(padded_taps[group], total_rows, my_start, rows_dev, count)
            matrix = jnp.where(allowed, matrix, jnp.zeros((), matrix.dtype))
            parts_out.append(
                jnp.dot(
                    matrix,
                    piece[:, group * GW : (group + 1) * GW],
                    preferred_element_type=jnp.float32,
                )
            )
        return total + jnp.concatenate(parts_out, axis=1)

    return lax.cond(needed, work, lambda total: total, empty)


def on_device(q_in, k_in, v_in, fir, skip, taps, segments, gain):
    rows_dev, width = q_in.shape
    stacked = jnp.stack([q_in, k_in, v_in])
    before = shifted(stacked[:, rows_dev - 2 :, :], "ctx", 1)
    padded = jnp.concatenate([before, stacked], axis=1).astype(jnp.float32)
    filtered = (
        fir[:, 0, None, :] * padded[:, 2:]
        + fir[:, 1, None, :] * padded[:, 1:-1]
        + fir[:, 2, None, :] * padded[:, :-2]
    )
    product_kv = (filtered[1] * filtered[2]).astype(jnp.bfloat16)
    all_segs = lax.all_gather(segments, "ctx", axis=0, tiled=True)
    conv = token_conv(product_kv, taps, all_segs, segments)
    gated = filtered[0] * (conv + skip * product_kv.astype(jnp.float32))
    squares = lax.psum(jnp.sum(gated * gated, axis=1), "grp")
    mixed = gated * lax.rsqrt(squares[:, None] / D + 1e-06) * gain
    return mixed.astype(jnp.bfloat16)


def solution(mesh):
    return jax.shard_map(
        on_device,
        mesh=mesh,
        in_specs=(
            P("ctx", "grp"),
            P("ctx", "grp"),
            P("ctx", "grp"),
            P(None, None, "grp"),
            P("grp"),
            P("grp", None),
            P("ctx"),
            P("grp"),
        ),
        out_specs=P("ctx", "grp"),
        check_vma=False,
    )
```

profile of v0, /device:TPU:2, one launch (start us, length us, event | category | flops | bytes accessed | tf_op | source)
XLA Modules:
  0.0 115.2 jit_solution(7496650928341975166)
XLA Ops:
  6.5 0.0 all-gather.4.cloned.1.call-start
  6.5 0.7 pad_maximum_fusion.13
  7.3 3.4 %collective-permute-start = (bf16[3,2,512]{2,1,0:T(2,128)(2,1)S(1)}, bf16[3,2,512]{2,1,0:T(2,128)(2,1)S(1)}, u32[]{:S(2)}, u32[]{:S(2)}) collective-permute-start(bf16[3,2,512]{2,1,0:T(2,128)(2,1)S(1)} %pad_maximum_fusion.13), channel_id=1, source_target_pairs={{0,16},{16,32},{32,48},{48,64},{64,80},{80,96},{96,112},{112,128},... | collective-permute-start | bytes 18440 | tf_op jit(solution)/shard_map/ppermute | solution.py:13
  10.7 0.9 fusion.33
  11.6 1.2 %collective-permute-done = bf16[3,2,512]{2,1,0:T(2,128)(2,1)S(1)} collective-permute-done((bf16[3,2,512]{2,1,0:T(2,128)(2,1)S(1)}, bf16[3,2,512]{2,1,0:T(2,128)(2,1)S(1)}, u32[]{:S(2)}, u32[]{:S(2)}) %collective-permute-start) | collective-permute-done | bytes 6176 | tf_op jit(solution)/shard_map/ppermute | solution.py:13
  12.8 1.1 maximum_convert_fusion
  14.0 0.0 copy-start.3
  14.0 0.0 copy-start
  14.0 0.2 fusion.28
  14.2 0.7 fusion.30
  14.9 0.0 all-gather.4.cloned.1.call-update
  14.9 0.0 copy-done.3
  15.0 20.9 %all-gather.1 = s32[16,1,128]{2,1,0:T(1,128)S(1)} all-gather(s32[1,1,128]{2,1,0:T(1,128)S(1)} %bitcast.55), channel_id=1, replica_groups=mesh['ctx'=16,'grp'=16] {'ctx'}, dimensions={0}, use_global_device_ids=true | all-gather | bytes 8704 | tf_op jit(solution)/shard_map/all_gather | solution.py:65
  35.9 0.6 slice.112
  37.1 0.1 slice_reduce_fusion
  37.3 30.4 %all-gather.4.cloned.1.call-done = bf16[1,2048,512]{2,1,0:T(8,128)(2,1)} async-done(((bf16[1,128,512]{2,1,0:T(8,128)(2,1)}), bf16[1,2048,512]{2,1,0:T(8,128)(2,1)}) %all-gather.4.cloned.1.call-update) | async-done | bytes 2097168 | tf_op jit(solution)/shard_map/all_gather | solution.py:32
  67.7 14.3 %conditional.1 = (f32[128,512]{1,0:T(8,128)S(1)}) conditional(s32[]{:T(128)} %convert_element_type.19, () %tuple.11, (s32[128]{0:T(128)S(1)}, s32[2048]{0:T(1024)S(1)}, s32[]{:T(128)}, bf16[6144]{0:T(1024)(128)(2,1)S(1)}, bf16[2048,512]{1,0:T(8,128)(2,1)}, /*index=5*/bf16[6144]{0:T(1024)(128)(2,1)S(1)}, bf16[6144]{0:T(1024)(128)(2,1)S(1)}, ...), branch_computations={%region_0.0_spmd, %region_1.2_spmd} | conditional | flops 270759680 | bytes 16835618 | solution.py:51
  67.7 0.1 dynamic_slice.8
  67.8 0.1 reverse.3
  67.9 0.1 slice.168
  67.9 0.1 dynamic_slice.9
  68.0 0.1 reverse.2
  68.1 0.1 slice.167
  68.2 0.1 pad_maximum_fusion.3
  68.3 0.1 dynamic_slice.10
  68.4 0.1 dynamic_slice.11
  68.4 0.1 reverse
  68.6 0.1 slice.165
  68.6 0.1 reverse.1
  68.7 0.1 slice.166
  68.8 0.1 pad_maximum_fusion.1
  68.9 0.6 tile.7
  69.6 1.0 reshape.26
  70.5 1.6 %fusion.3 = f32[128,128]{0,1:T(8,128)S(1)} fusion(bf16[128,2175]{1,0:T(8,128)(2,1)S(1)} %reshape.26, bf16[2048,512]{1,0:T(8,128)(2,1)} %get-tuple-element.31, s32[2048]{0:T(1024)S(1)} %get-tuple-element.28, s32[128]{0:T(128)S(1)} %get-tuple-element.27), kind=kOutput, calls=%fused_computation.7 | convolution fusion | flops 67633152 | bytes 1122816 | tf_op jit(solution)/shard_map/cond/branch_1_fun/dot_general | solution.py:43
  72.2 0.6 tile.3
  72.8 1.0 reshape.24
  73.8 1.6 %fusion.1 = f32[128,128]{0,1:T(8,128)S(1)} fusion(bf16[128,2175]{1,0:T(8,128)(2,1)S(1)} %reshape.24, bf16[2048,512]{1,0:T(8,128)(2,1)} %get-tuple-element.31, s32[2048]{0:T(1024)S(1)} %get-tuple-element.28, s32[128]{0:T(128)S(1)} %get-tuple-element.27), kind=kOutput, calls=%fused_computation.5 | convolution fusion | flops 67633152 | bytes 1122816 | tf_op jit(solution)/shard_map/cond/branch_1_fun/dot_general | solution.py:43
  75.4 0.6 tile.5
  76.0 1.0 reshape.25
  77.0 1.6 %fusion.2 = f32[128,128]{0,1:T(8,128)S(1)} fusion(bf16[128,2175]{1,0:T(8,128)(2,1)S(1)} %reshape.25, bf16[2048,512]{1,0:T(8,128)(2,1)} %get-tuple-element.31, s32[2048]{0:T(1024)S(1)} %get-tuple-element.28, s32[128]{0:T(128)S(1)} %get-tuple-element.27), kind=kOutput, calls=%fused_computation.6 | convolution fusion | flops 67633152 | bytes 1122816 | tf_op jit(solution)/shard_map/cond/branch_1_fun/dot_general | solution.py:43
  78.6 0.6 tile.1
  79.2 1.0 reshape.23
  80.2 1.6 %fusion = f32[128,128]{0,1:T(8,128)S(1)} fusion(bf16[128,2175]{1,0:T(8,128)(2,1)S(1)} %reshape.23, bf16[2048,512]{1,0:T(8,128)(2,1)} %get-tuple-element.31, s32[2048]{0:T(1024)S(1)} %get-tuple-element.28, s32[128]{0:T(128)S(1)} %get-tuple-element.27), kind=kOutput, calls=%fused_computation.4 | convolution fusion | flops 67633152 | bytes 1122816 | tf_op jit(solution)/shard_map/cond/branch_1_fun/dot_general | solution.py:43
  81.8 0.1 copy.13
  82.0 0.2 multiply_reduce_fusion
  82.1 25.5 %psum.7 = f32[128]{0:T(128)S(1)} all-reduce(f32[128]{0:T(128)S(1)} %multiply_reduce_fusion), channel_id=1, replica_groups=mesh['ctx'=16,'grp'=16] {'grp'}, use_global_device_ids=true, to_apply=%region_3.4 | all-reduce | flops 128 | bytes 1024 | tf_op jit(solution)/shard_map/psum | solution.py:68
  107.6 0.0 copy-done.2
  107.6 0.8 multiply_convert_fusion
  (14 shorter events, 0.2 us)
Async XLA Ops:
  6.5 61.1 %all-gather.4.cloned.1.call-start = ((), (), s32[]{:S(2)}) async-start(), calls=%async_computation | async-start | bytes 2228224 | tf_op jit(solution)/shard_map/all_gather | solution.py:32
  7.3 5.5 %collective-permute-start = (bf16[3,2,512]{2,1,0:T(2,128)(2,1)S(1)}, bf16[3,2,512]{2,1,0:T(2,128)(2,1)S(1)}, u32[]{:S(2)}, u32[]{:S(2)}) collective-permute-start(bf16[3,2,512]{2,1,0:T(2,128)(2,1)S(1)} %pad_maximum_fusion.13), channel_id=1, source_target_pairs={{0,16},{16,32},{32,48},{48,64},{64,80},{80,96},{96,112},{112,128},... | collective-permute-start | bytes 18440 | tf_op jit(solution)/shard_map/ppermute | solution.py:13
  14.0 1.0 copy-start.3
  14.0 23.1 %copy-start = (bf16[4,2048]{1,0:T(4,128)(2,1)S(1)}, bf16[4,2048]{1,0:T(4,128)(2,1)}, u32[]{:S(2)}) copy-start(bf16[4,2048]{1,0:T(4,128)(2,1)} %param.15) | copy-start | bytes 49156
  67.7 14.3 %copy-start.1 = (f32[512]{0:T(512)S(1)}, f32[512]{0:T(512)}, u32[]{:S(2)}) copy-start(f32[512]{0:T(512)} %param.14) | copy-start | bytes 6148
  67.7 39.9 %copy-start.2 = (f32[512]{0:T(512)S(1)}, f32[512]{0:T(512)}, u32[]{:S(2)}) copy-start(f32[512]{0:T(512)} %param.17) | copy-start | bytes 6148
Sparse Core Ops, SparseCore 0:
  15.1 52.5 all-gather.3
where the time goes:
time: 116 us; the launch traced here: 115 us
  blocking collectives  46.4 us (40%)
  waiting for transfers between devices  31.7 us (27%)
  between operations  14.1 us (12%)
  local copies, waits for them, and re-layouts  9.3 us (8%)
  matrix products  6.31 us (5%)
  other arithmetic  3.91 us (3%)
  starting transfers between devices  3.4 us (3%)
    all_gather x1, waiting for transfers between devices, token_conv(): piece = lax.all_gather(product_kv, 'ctx', axis=0, tiled=True)  30.4 us
    psum x1, blocking collectives, on_device(): squares = lax.psum(jnp.sum(gated * gated, axis=1), 'grp')  25.5 us
    all_gather x1, blocking collectives, on_device(): all_segs = lax.all_gather(segments, 'ctx', axis=0, tiled=True)  20.9 us
    dot_general x4, matrix products, work(): jnp.dot(matrix, piece[:, group * GW:(group + 1) * GW], preferred_element_...  6.31 us
    reshape x4, local copies, waits for them, and re-layouts, band_rect(): tiled = jnp.tile(flipped, rows)[:rows * length].reshape(rows, length)  3.87 us
    ppermute x1, starting transfers between devices, shifted(): return lax.ppermute(value, axis, pairs)  3.4 us
    another operation x8, local copies, waits for them, and re-layouts, band_rect(): tiled = jnp.tile(flipped, rows)[:rows * length].reshape(rows, length)  2.64 us
  transfers between devices with their start and end apart: 2, of which 2 were waited for; matrix products, arithmetic and copies ran while one was open for 1% of the time, Pallas kernels for 0%

commit v1 on v0

--- a/solution.py
+++ b/solution.py
@@ -65,7 +65,7 @@
     all_segs = lax.all_gather(segments, "ctx", axis=0, tiled=True)
     conv = token_conv(product_kv, taps, all_segs, segments)
     gated = filtered[0] * (conv + skip * product_kv.astype(jnp.float32))
-    squares = lax.psum(jnp.sum(gated * gated, axis=1), "grp")
+    squares = jnp.sum(lax.all_gather(jnp.sum(gated * gated, axis=1), "grp"), axis=0)
     mixed = gated * lax.rsqrt(squares[:, None] / D + 1e-06) * gain
     return mixed.astype(jnp.bfloat16)
 

time: 116 us -> 109 us (0.940)
  blocking collectives: 46.4 us -> 38.3 us
    psum x1 -> x0, blocking collectives: 25.5 us -> none  [on_device(): squares = lax.psum(jnp.sum(gated * gated, axis=1), 'grp')]
    all_gather x0 -> x1, blocking collectives: none -> 17.3 us  [on_device(): lax.all_gather(jnp.sum(gated * gated, axis=1), 'grp')]
where the time goes in v1:
time: 109 us; the launch traced here: 107 us
  blocking collectives  38.3 us (35%)
  waiting for transfers between devices  31.7 us (29%)
  between operations  14.1 us (13%)
  local copies, waits for them, and re-layouts  9.3 us (9%)
  matrix products  6.31 us (6%)
  other arithmetic  3.95 us (4%)
  starting transfers between devices  3.4 us (3%)
    all_gather x1, waiting for transfers between devices, token_conv(): piece = lax.all_gather(product_kv, 'ctx', axis=0, tiled=True)  30.4 us
    all_gather x1, blocking collectives, on_device(): all_segs = lax.all_gather(segments, 'ctx', axis=0, tiled=True)  20.9 us
    all_gather x1, blocking collectives, on_device(): lax.all_gather(jnp.sum(gated * gated, axis=1), 'grp')  17.3 us
    dot_general x4, matrix products, work(): jnp.dot(matrix, piece[:, group * GW:(group + 1) * GW], preferred_element_...  6.31 us
    reshape x4, local copies, waits for them, and re-layouts, band_rect(): tiled = jnp.tile(flipped, rows)[:rows * length].reshape(rows, length)  3.87 us
    ppermute x1, starting transfers between devices, shifted(): return lax.ppermute(value, axis, pairs)  3.4 us
    another operation x8, local copies, waits for them, and re-layouts, band_rect(): tiled = jnp.tile(flipped, rows)[:rows * length].reshape(rows, length)  2.64 us
  transfers between devices with their start and end apart: 2, of which 2 were waited for; matrix products, arithmetic and copies ran while one was open for 1% of the time, Pallas kernels for 0%

profile of v1, /device:TPU:2, one launch (start us, length us, event | category | flops | bytes accessed | tf_op | source)
XLA Modules:
  0.0 107.1 jit_solution(4552383848232299369)
XLA Ops:
  6.5 0.0 all-gather.6.cloned.1.call-start
  6.5 0.7 pad_maximum_fusion.13
  7.3 3.4 %collective-permute-start = (bf16[3,2,512]{2,1,0:T(2,128)(2,1)S(1)}, bf16[3,2,512]{2,1,0:T(2,128)(2,1)S(1)}, u32[]{:S(2)}, u32[]{:S(2)}) collective-permute-start(bf16[3,2,512]{2,1,0:T(2,128)(2,1)S(1)} %pad_maximum_fusion.13), channel_id=1, source_target_pairs={{0,16},{16,32},{32,48},{48,64},{64,80},{80,96},{96,112},{112,128},... | collective-permute-start | bytes 18440 | tf_op jit(solution)/shard_map/ppermute | solution.py:13
  10.7 0.9 fusion.33
  11.6 1.2 %collective-permute-done = bf16[3,2,512]{2,1,0:T(2,128)(2,1)S(1)} collective-permute-done((bf16[3,2,512]{2,1,0:T(2,128)(2,1)S(1)}, bf16[3,2,512]{2,1,0:T(2,128)(2,1)S(1)}, u32[]{:S(2)}, u32[]{:S(2)}) %collective-permute-start) | collective-permute-done | bytes 6176 | tf_op jit(solution)/shard_map/ppermute | solution.py:13
  12.8 1.1 %maximum_convert_fusion = f32[3,130,512]{2,1,0:T(8,128)S(1)} fusion(bf16[1,128,512]{2,1,0:T(8,128)(2,1)} %bitcast.44, bf16[1,128,512]{2,1,0:T(8,128)(2,1)} %bitcast.46, bf16[1,128,512]{2,1,0:T(8,128)(2,1)} %bitcast.48, bf16[3,2,512]{2,1,0:T(2,128)(2,1)S(1)} %collective-permute-done), kind=kLoop, calls=%fused_computation.42 | loop fusion | flops 1597440 | bytes 1198080 | tf_op jit(solution)/shard_map/convert_element_type | solution.py:58
  14.0 0.0 copy-start.3
  14.0 0.0 copy-start
  14.0 0.2 fusion.28
  14.2 0.7 fusion.30
  14.9 0.0 all-gather.6.cloned.1.call-update
  14.9 0.0 copy-done.3
  15.0 20.9 %all-gather.2 = s32[16,1,128]{2,1,0:T(1,128)S(1)} all-gather(s32[1,1,128]{2,1,0:T(1,128)S(1)} %bitcast.57), channel_id=1, replica_groups=mesh['ctx'=16,'grp'=16] {'ctx'}, dimensions={0}, use_global_device_ids=true | all-gather | bytes 8704 | tf_op jit(solution)/shard_map/all_gather | solution.py:65
  35.9 0.6 slice.112
  37.1 0.0 copy-done
  37.1 0.1 slice_reduce_fusion
  37.3 30.4 %all-gather.6.cloned.1.call-done = bf16[1,2048,512]{2,1,0:T(8,128)(2,1)} async-done(((bf16[1,128,512]{2,1,0:T(8,128)(2,1)}), bf16[1,2048,512]{2,1,0:T(8,128)(2,1)}) %all-gather.6.cloned.1.call-update) | async-done | bytes 2097168 | tf_op jit(solution)/shard_map/all_gather | solution.py:32
  67.7 14.3 %conditional.1 = (f32[128,512]{1,0:T(8,128)S(1)}) conditional(s32[]{:T(128)} %convert_element_type.19, () %tuple.11, (s32[128]{0:T(128)S(1)}, s32[2048]{0:T(1024)S(1)}, s32[]{:T(128)}, bf16[6144]{0:T(1024)(128)(2,1)S(1)}, bf16[2048,512]{1,0:T(8,128)(2,1)}, /*index=5*/bf16[6144]{0:T(1024)(128)(2,1)S(1)}, bf16[6144]{0:T(1024)(128)(2,1)S(1)}, ...), branch_computations={%region_0.0_spmd, %region_1.2_spmd} | conditional | flops 270759680 | bytes 16835618 | solution.py:51
  67.7 0.1 dynamic_slice.8
  67.8 0.1 reverse.3
  67.9 0.1 slice.168
  67.9 0.1 dynamic_slice.9
  68.0 0.1 reverse.2
  68.1 0.1 slice.167
  68.2 0.1 pad_maximum_fusion.3
  68.3 0.1 dynamic_slice.10
  68.4 0.1 dynamic_slice.11
  68.4 0.1 reverse
  68.6 0.1 slice.165
  68.6 0.1 reverse.1
  68.7 0.1 slice.166
  68.8 0.1 pad_maximum_fusion.1
  68.9 0.6 tile.7
  69.6 1.0 reshape.30
  70.5 1.6 %fusion.3 = f32[128,128]{0,1:T(8,128)S(1)} fusion(bf16[128,2175]{1,0:T(8,128)(2,1)S(1)} %reshape.30, bf16[2048,512]{1,0:T(8,128)(2,1)} %get-tuple-element.31, s32[2048]{0:T(1024)S(1)} %get-tuple-element.28, s32[128]{0:T(128)S(1)} %get-tuple-element.27), kind=kOutput, calls=%fused_computation.7 | convolution fusion | flops 67633152 | bytes 1122816 | tf_op jit(solution)/shard_map/cond/branch_1_fun/dot_general | solution.py:43
  72.2 0.6 tile.3
  72.8 1.0 reshape.28
  73.8 1.6 %fusion.1 = f32[128,128]{0,1:T(8,128)S(1)} fusion(bf16[128,2175]{1,0:T(8,128)(2,1)S(1)} %reshape.28, bf16[2048,512]{1,0:T(8,128)(2,1)} %get-tuple-element.31, s32[2048]{0:T(1024)S(1)} %get-tuple-element.28, s32[128]{0:T(128)S(1)} %get-tuple-element.27), kind=kOutput, calls=%fused_computation.5 | convolution fusion | flops 67633152 | bytes 1122816 | tf_op jit(solution)/shard_map/cond/branch_1_fun/dot_general | solution.py:43
  75.4 0.6 tile.5
  76.0 1.0 reshape.29
  77.0 1.6 %fusion.2 = f32[128,128]{0,1:T(8,128)S(1)} fusion(bf16[128,2175]{1,0:T(8,128)(2,1)S(1)} %reshape.29, bf16[2048,512]{1,0:T(8,128)(2,1)} %get-tuple-element.31, s32[2048]{0:T(1024)S(1)} %get-tuple-element.28, s32[128]{0:T(128)S(1)} %get-tuple-element.27), kind=kOutput, calls=%fused_computation.6 | convolution fusion | flops 67633152 | bytes 1122816 | tf_op jit(solution)/shard_map/cond/branch_1_fun/dot_general | solution.py:43
  78.6 0.6 tile.1
  79.2 1.0 reshape.27
  80.2 1.6 %fusion = f32[128,128]{0,1:T(8,128)S(1)} fusion(bf16[128,2175]{1,0:T(8,128)(2,1)S(1)} %reshape.27, bf16[2048,512]{1,0:T(8,128)(2,1)} %get-tuple-element.31, s32[2048]{0:T(1024)S(1)} %get-tuple-element.28, s32[128]{0:T(128)S(1)} %get-tuple-element.27), kind=kOutput, calls=%fused_computation.4 | convolution fusion | flops 67633152 | bytes 1122816 | tf_op jit(solution)/shard_map/cond/branch_1_fun/dot_general | solution.py:43
  81.8 0.1 copy.13
  82.0 0.2 multiply_reduce_fusion
  82.1 17.3 %all-gather.3 = f32[16,1,128]{2,1,0:T(1,128)S(1)} all-gather(f32[1,1,128]{2,1,0:T(1,128)S(1)} %bitcast.56), channel_id=3, replica_groups=mesh['ctx'=16,'grp'=16] {'grp'}, dimensions={0}, use_global_device_ids=true | all-gather | bytes 8704 | tf_op jit(solution)/shard_map/all_gather | solution.py:68
  99.5 0.8 multiply_convert_fusion
  (15 shorter events, 0.3 us)
Async XLA Ops:
  6.5 61.1 %all-gather.6.cloned.1.call-start = ((), (), s32[]{:S(2)}) async-start(), calls=%async_computation | async-start | bytes 2228224 | tf_op jit(solution)/shard_map/all_gather | solution.py:32
  7.3 5.5 %collective-permute-start = (bf16[3,2,512]{2,1,0:T(2,128)(2,1)S(1)}, bf16[3,2,512]{2,1,0:T(2,128)(2,1)S(1)}, u32[]{:S(2)}, u32[]{:S(2)}) collective-permute-start(bf16[3,2,512]{2,1,0:T(2,128)(2,1)S(1)} %pad_maximum_fusion.13), channel_id=1, source_target_pairs={{0,16},{16,32},{32,48},{48,64},{64,80},{80,96},{96,112},{112,128},... | collective-permute-start | bytes 18440 | tf_op jit(solution)/shard_map/ppermute | solution.py:13
  14.0 1.0 copy-start.3
  14.0 23.1 %copy-start = (bf16[4,2048]{1,0:T(4,128)(2,1)S(1)}, bf16[4,2048]{1,0:T(4,128)(2,1)}, u32[]{:S(2)}) copy-start(bf16[4,2048]{1,0:T(4,128)(2,1)} %param.15) | copy-start | bytes 49156
  67.7 14.3 %copy-start.1 = (f32[512]{0:T(512)S(1)}, f32[512]{0:T(512)}, u32[]{:S(2)}) copy-start(f32[512]{0:T(512)} %param.14) | copy-start | bytes 6148
  67.7 31.8 %copy-start.2 = (f32[512]{0:T(512)S(1)}, f32[512]{0:T(512)}, u32[]{:S(2)}) copy-start(f32[512]{0:T(512)} %param.17) | copy-start | bytes 6148
Sparse Core Ops, SparseCore 0:
  15.1 52.5 all-gather.5
